TPU v7x, 128 devices: a whole 4x4x4 slice. The times are simulated.
128 devices in a mesh: shot: 4 (over z), row: 8 (over x, y_lo), col: 4 (over y_hi, core).
Axes of the slice: x: 4, y: 4 (y_hi: 2, y_lo: 2; y = y_hi * 2 + y_lo), z: 4, core: 2. Of those that a mesh axis runs over, the one named last changes fastest.
Arguments:
- velocity: float32 [256, 256, 384], P(('row', 'shot'), 'col'), may hold values from 1.5 to 4.5
- momentum: float32 [256, 256, 384], P(('row', 'shot'), 'col'), may hold values from -6 to 6
- mass_diag: float32 [256, 256, 384], P(('row', 'shot'), 'col'), may hold values from 0.5 to 2
- u_prev: float32 [4, 256, 256, 384], P('shot', 'row', 'col'), may hold values from -6 to 6
- u_cur: float32 [4, 256, 256, 384], P('shot', 'row', 'col'), may hold values from -6 to 6
- adj_next: float32 [4, 256, 256, 384], P('shot', 'row', 'col'), may hold values from -6 to 6
- adj_cur: float32 [4, 256, 256, 384], P('shot', 'row', 'col'), may hold values from -6 to 6
- observed: float32 [4, 2, 256, 256], P('shot', None, 'row', 'col'), may hold values from -6 to 6
- rec_depth: int32 [4, 256, 256], P('shot', 'row', 'col'), may hold values from 0 to 383
- src_cell: int32 [4, 3], P('shot'), may hold values from 0 to 255
- wavelet: float32 [4, 2], P('shot'), may hold values from -60 to 60
Outputs:
- v_new: float32 [256, 256, 384], P(('row', 'shot'), 'col')
- p_half: float32 [256, 256, 384], P(('row', 'shot'), 'col')
All inputs are finite; a program needn't handle non-finite values.
Results may differ from a plain program's by a relative error of at most 0.0001.
Values sent between devices are 32-bit elements; how exact they have to be, the bound alone decides.
A program may use at most 128 MiB of HBM per device.

v0:
```python
import jax
import jax.numpy as jnp
from jax import lax
from jax.sharding import PartitionSpec as P

STENCIL = (-205.0 / 72.0, 8.0 / 5.0, -1.0 / 5.0, 8.0 / 315.0, -1.0 / 560.0)
squared_courant = 0.012
leap_step = 0.2


def extended(block, sides, width):
    for axis, dim in sides:
        count = lax.axis_size(axis)
        forward = [(i, i + 1) for i in range(count - 1)]
        backward = [(target, source) for source, target in forward]
        low = lax.ppermute(
            lax.slice_in_dim(block, block.shape[dim] - width, None, axis=dim), axis, forward
        )
        high = lax.ppermute(lax.slice_in_dim(block, 0, width, axis=dim), axis, backward)
        block = jnp.concatenate([low, block, high], axis=dim)
    return block


def laplace(padded):
    row_count = padded.shape[0] - 8
    col_count = padded.shape[1] - 8
    depth_cells = padded.shape[2]
    center = padded[4 : 4 + row_count, 4 : 4 + col_count]
    z_padded = jnp.pad(center, ((0, 0), (0, 0), (4, 4)))
    result = 3.0 * STENCIL[0] * center
    for offset in range(1, 5):
        along = (
            padded[4 + offset : 4 + offset + row_count, 4 : 4 + col_count]
            + padded[4 - offset : 4 - offset + row_count, 4 : 4 + col_count]
        )
        along = (
            along
            + padded[4 : 4 + row_count, 4 + offset : 4 + offset + col_count]
            + padded[4 : 4 + row_count, 4 - offset : 4 - offset + col_count]
        )
        along = (
            along
            + z_padded[:, :, 4 + offset : 4 + offset + depth_cells]
            + z_padded[:, :, 4 - offset : 4 - offset + depth_cells]
        )
        result = result + STENCIL[offset] * along
    return result


def with_faces(field):
    return extended(field, (("row", 0), ("col", 1)), 4)


def on_device(
    velocity,
    momentum,
    mass_diag,
    u_prev,
    u_cur,
    adj_next,
    adj_cur,
    observed,
    rec_depth,
    src_cell,
    wavelet,
):
    full_velocity = lax.all_gather(velocity, "shot", axis=0, tiled=True)
    stiffness = squared_courant * full_velocity * full_velocity
    row_count, col_count, depth_cells = full_velocity.shape
    oldest = u_prev[0]
    present = u_cur[0]
    adj_later = adj_next[0]
    adj_now = adj_cur[0]
    padded_wave = extended(present, (("row", 0), ("col", 1)), 4)
    padded_adjoint = extended(adj_now, (("row", 0), ("col", 1)), 4)
    x_index = lax.iota(jnp.int32, row_count) + lax.axis_index("row") * row_count
    y_index = lax.iota(jnp.int32, col_count) + lax.axis_index("col") * col_count
    z_index = lax.iota(jnp.int32, depth_cells)
    cell = src_cell[0]
    source_mask = (
        (x_index == cell[0])[:, None, None]
        & (y_index == cell[1])[None, :, None]
        & (z_index == cell[2])[None, None, :]
    ).astype(jnp.float32)
    advanced = (
        2.0 * present - oldest + stiffness * laplace(padded_wave) + wavelet[0, 0] * source_mask
    )
    farthest = (
        2.0 * advanced
        - present
        + stiffness * laplace(with_faces(advanced))
        + wavelet[0, 1] * source_mask
    )
    receiver_mask = (z_index[None, None, :] == rec_depth[0][:, :, None]).astype(jnp.float32)
    misfit_late = jnp.sum(farthest * receiver_mask, axis=2) - observed[0, 1]
    misfit_early = jnp.sum(advanced * receiver_mask, axis=2) - observed[0, 0]
    adj_two = (
        2.0 * adj_now
        - adj_later
        + stiffness * laplace(padded_adjoint)
        + misfit_late[:, :, None] * receiver_mask
    )
    adj_one = (
        2.0 * adj_two
        - adj_now
        + stiffness * laplace(with_faces(adj_two))
        + misfit_early[:, :, None] * receiver_mask
    )
    imaging = adj_two * (farthest - 2.0 * advanced + present) + adj_one * (
        advanced - 2.0 * present + oldest
    )
    share_rows = velocity.shape[0]
    full_sum = lax.psum(imaging, "shot")
    summed = lax.dynamic_slice_in_dim(full_sum, lax.axis_index("shot") * share_rows, share_rows, 0)
    gradient = 2.0 / velocity * summed
    p_half = momentum - 0.5 * leap_step * gradient
    v_new = velocity + leap_step * p_half / mass_diag
    return (v_new, p_half)


def solution(mesh):
    return jax.shard_map(
        on_device,
        mesh=mesh,
        in_specs=(
            P(("row", "shot"), "col", None),
            P(("row", "shot"), "col", None),
            P(("row", "shot"), "col", None),
            P("shot", "row", "col", None),
            P("shot", "row", "col", None),
            P("shot", "row", "col", None),
            P("shot", "row", "col", None),
            P("shot", None, "row", "col"),
            P("shot", "row", "col"),
            P("shot", None),
            P("shot", None),
        ),
        out_specs=(P(("row", "shot"), "col", None), P(("row", "shot"), "col", None)),
        check_vma=False,
    )
```

profile of v0, /device:TPU:1, one launch (start us, length us, event | category | flops | bytes accessed | tf_op | source)
XLA Modules:
  0.0 376.6 jit_solution(13717517673409891883)
XLA Ops:
  7.2 0.0 copy-start
  7.2 0.0 all-gather.2.cloned.1.call-start
  7.2 0.7 all-gather.2.cloned.1.call-update
  7.9 0.0 all-reduce.6.cloned.1.call-start
  8.0 2.2 slice_bitcast_fusion.3
  10.2 1.3 collective-permute-start
  11.5 5.4 %collective-permute-start.1 = (f32[4,64,384]{2,1,0:T(8,128)}, f32[4,64,384]{2,1,0:T(8,128)}, u32[]{:S(2)}, u32[]{:S(2)}) collective-permute-start(f32[4,64,384]{2,1,0:T(8,128)} %get-tuple-element.30), channel_id=1, source_target_pairs={{0,4},{4,8},{8,12},{12,16},{16,20},{20,24},{24,28},{1,5},{5,9},{9,... | collective-permute-start | bytes 1179656 | tf_op jit(solution)/shard_map/ppermute | solution.py:16
  16.9 2.1 slice_bitcast_fusion.1
  19.0 1.3 collective-permute-start.4
  20.3 4.9 %collective-permute-start.5 = (f32[4,64,384]{2,1,0:T(8,128)}, f32[4,64,384]{2,1,0:T(8,128)}, u32[]{:S(2)}, u32[]{:S(2)}) collective-permute-start(f32[4,64,384]{2,1,0:T(8,128)} %get-tuple-element.28), channel_id=1, source_target_pairs={{0,4},{4,8},{8,12},{12,16},{16,20},{20,24},{24,28},{1,5},{5,9},{9,... | collective-permute-start | bytes 1179656 | tf_op jit(solution)/shard_map/ppermute | solution.py:16
  25.2 0.7 fusion.146
  25.9 0.6 iota_compare_fusion.1
  26.5 0.6 add_compare_fusion.1
  27.1 0.6 fusion.145
  27.7 3.3 collective-permute-done.4
  31.0 18.5 %collective-permute-done.5 = f32[4,64,384]{2,1,0:T(8,128)} collective-permute-done((f32[4,64,384]{2,1,0:T(8,128)}, f32[4,64,384]{2,1,0:T(8,128)}, u32[]{:S(2)}, u32[]{:S(2)}) %collective-permute-start.5) | collective-permute-done | bytes 393248 | tf_op jit(solution)/shard_map/ppermute | solution.py:16
  49.5 1.0 pad_maximum_fusion.20
  50.5 2.4 collective-permute-start.6
  52.9 4.7 %collective-permute-start.7 = (f32[40,4,384]{2,1,0:T(4,128)S(1)}, f32[40,4,384]{2,1,0:T(4,128)S(1)}, u32[]{:S(2)}, u32[]{:S(2)}) collective-permute-start(f32[40,4,384]{2,1,0:T(4,128)S(1)} %get-tuple-element.18), channel_id=1, source_target_pairs={{0,1},{1,2},{2,3},{4,5},{5,6},{6,7},{8,9},{9,10},{10,11},{12,13},{... | collective-permute-start | bytes 737288 | tf_op jit(solution)/shard_map/ppermute | solution.py:16
  57.6 0.7 add_compare_fusion
  58.3 0.1 broadcast_and_fusion
  58.3 1.2 collective-permute-done.6
  59.5 1.2 collective-permute-done.7
  60.7 5.9 %pad_maximum_fusion.1 = (f32[40,68,384]{2,1,0:T(8,128)}, f32[40,68,384]{2,1,0:T(8,128)}) fusion(f32[40,4,384]{2,1,0:T(4,128)S(1)} %collective-permute-done.6, f32[4,64,384]{2,1,0:T(8,128)} %collective-permute-done.4, f32[32,64,384]{2,1,0:T(8,128)S(1)} %bitcast.36, f32[4,64,384]{2,1,0:T(8,128)} %collective-permute-done.5, ...), kind=kLoop, calls=%fused_computation.59 | loop fusion | flops 6266880 | bytes 12779520 | tf_op jit(solution)/shard_map/concatenate | solution.py:20
  66.6 23.5 %fusion.75 = f32[32,64,384]{2,1,0:T(8,128)} fusion(f32[32,64,384]{2,1,0:T(8,128)S(1)} %bitcast.37, f32[4,64,384]{2,1,0:T(8,128)} %collective-permute-done.5, f32[4,64,384]{2,1,0:T(8,128)} %collective-permute-done.4, f32[40,68,384]{2,1,0:T(8,128)} %get-tuple-element.16, f32[40,68,384]{2,1,0:T(8,128)} %get-tuple-element.15, f32[1,32,64,384]{3,2,1,0:T(8,128)} %param.14, ...), kind=kLoop, calls=%fused_computation.166 | loop fusion | flops 36175872 | bytes 38537604 | tf_op jit(solution)/shard_map/add | solution.py:86
  90.1 1.3 fusion.144
  91.5 4.1 %collective-permute-start.9 = (f32[4,64,384]{2,1,0:T(8,128)S(1)}, f32[4,64,384]{2,1,0:T(8,128)S(1)}, u32[]{:S(2)}, u32[]{:S(2)}) collective-permute-start(f32[4,64,384]{2,1,0:T(8,128)S(1)} %get-tuple-element.25), channel_id=1, source_target_pairs={{0,4},{4,8},{8,12},{12,16},{16,20},{20,24},{24,28},{1,5},{5,9},{9,... | collective-permute-start | bytes 1179656 | tf_op jit(solution)/shard_map/ppermute | solution.py:16
  95.6 1.3 collective-permute-start.8
  96.9 0.0 collective-permute-done
  96.9 0.0 collective-permute-done.1
  96.9 1.2 pad_maximum_fusion.23
  98.1 0.0 copy-start.3
  98.2 2.2 collective-permute-start.2
  100.3 6.8 %collective-permute-start.3 = (f32[40,4,384]{2,1,0:T(4,128)S(1)}, f32[40,4,384]{2,1,0:T(4,128)S(1)}, u32[]{:S(2)}, u32[]{:S(2)}) collective-permute-start(f32[40,4,384]{2,1,0:T(4,128)S(1)} %get-tuple-element.22), channel_id=1, source_target_pairs={{0,1},{1,2},{2,3},{4,5},{5,6},{6,7},{8,9},{9,10},{10,11},{12,13},{... | collective-permute-start | bytes 737288 | tf_op jit(solution)/shard_map/ppermute | solution.py:16
  107.1 2.0 collective-permute-done.9
  109.1 0.0 collective-permute-done.8
  109.2 0.1 pad_maximum_fusion.17
  109.2 1.9 collective-permute-start.10
  111.2 5.3 %collective-permute-start.11 = (f32[40,4,384]{2,1,0:T(4,128)S(1)}, f32[40,4,384]{2,1,0:T(4,128)S(1)}, u32[]{:S(2)}, u32[]{:S(2)}) collective-permute-start(f32[40,4,384]{2,1,0:T(4,128)S(1)} %get-tuple-element.14), channel_id=1, source_target_pairs={{0,1},{1,2},{2,3},{4,5},{5,6},{6,7},{8,9},{9,10},{10,11},{12,13},{... | collective-permute-start | bytes 737288 | tf_op jit(solution)/shard_map/ppermute | solution.py:16
  116.5 5.8 %pad_maximum_fusion = (f32[40,68,384]{2,1,0:T(8,128)}, f32[40,68,384]{2,1,0:T(8,128)}) fusion(f32[40,4,384]{2,1,0:T(4,128)S(1)} %collective-permute-done.2, f32[4,64,384]{2,1,0:T(8,128)S(1)} %collective-permute-done, f32[32,64,384]{2,1,0:T(8,128)S(1)} %bitcast.40, f32[4,64,384]{2,1,0:T(8,128)} %collective-permute-done.1, ...), kind=kLoop, calls=%fused_computation.57 | loop fusion | flops 6266880 | bytes 12779520 | tf_op jit(solution)/shard_map/concatenate | solution.py:20
  122.3 0.0 collective-permute-done.11
  122.4 4.7 %pad_maximum_fusion.2 = (f32[40,68,384]{2,1,0:T(8,128)}, f32[40,68,384]{2,1,0:T(8,128)}) fusion(f32[40,4,384]{2,1,0:T(4,128)S(1)} %collective-permute-done.10, f32[4,64,384]{2,1,0:T(8,128)S(1)} %collective-permute-done.8, f32[32,64,384]{2,1,0:T(8,128)S(1)} %copy-done.1, f32[4,64,384]{2,1,0:T(8,128)S(1)} %collective-permute-done.9, ...), kind=kLoop, calls=%fused_computation.61 | loop fusion | flops 6266880 | bytes 12779520 | tf_op jit(solution)/shard_map/concatenate | solution.py:20
  127.0 45.6 %select_reduce_fusion = (f32[32,64]{1,0:T(8,128)}, f32[32,64]{1,0:T(8,128)}, f32[32,64,384]{2,1,0:T(8,128)}) fusion(f32[32,64,384]{2,1,0:T(8,128)} %fusion.75, s32[32,64]{1,0:T(8,128)S(1)} %bitcast.41, f32[]{:T(128)} %bitcast.13, pred[384]{0:T(512)(128)(4,1)} %copy-done.15, pred[32,64]{1,0:T(8,128)(4,1)} %copy-done.13, ...), kind=kLoop, calls=%fused_computation.252 | loop fusion | flops 40103936 | bytes 38562180 | tf_op jit(solution)/shard_map/reduce_sum | solution.py:96
  172.6 1.4 bitcast_subtract_fusion.2
  174.0 43.2 %fusion.106 = f32[32,64,384]{2,1,0:T(8,128)} fusion(f32[32,64,384]{2,1,0:T(8,128)} %bitcast.39, f32[4,64,384]{2,1,0:T(8,128)} %collective-permute-done.1, f32[4,64,384]{2,1,0:T(8,128)S(1)} %collective-permute-done, f32[40,68,384]{2,1,0:T(8,128)} %get-tuple-element.20, f32[40,68,384]{2,1,0:T(8,128)} %get-tuple-element.19, f32[1,32,64,384]{3,2,1,0:T(8,128)} %param.16, ...), kind=kLoop, calls=%fused_computation.197 | loop fusion | flops 36175872 | bytes 38551552 | tf_op jit(solution)/shard_map/add | solution.py:98
  217.2 1.3 fusion.143
  218.5 1.3 collective-permute-start.12
  219.8 4.5 %collective-permute-start.13 = (f32[4,64,384]{2,1,0:T(8,128)S(1)}, f32[4,64,384]{2,1,0:T(8,128)S(1)}, u32[]{:S(2)}, u32[]{:S(2)}) collective-permute-start(f32[4,64,384]{2,1,0:T(8,128)S(1)} %get-tuple-element.24), channel_id=1, source_target_pairs={{0,4},{4,8},{8,12},{12,16},{16,20},{20,24},{24,28},{1,5},{5,9},{9,... | collective-permute-start | bytes 1179656 | tf_op jit(solution)/shard_map/ppermute | solution.py:16
  224.3 4.9 %collective-permute-done.12 = f32[4,64,384]{2,1,0:T(8,128)S(1)} collective-permute-done((f32[4,64,384]{2,1,0:T(8,128)S(1)}, f32[4,64,384]{2,1,0:T(8,128)S(1)}, u32[]{:S(2)}, u32[]{:S(2)}) %collective-permute-start.12) | collective-permute-done | bytes 393248 | tf_op jit(solution)/shard_map/ppermute | solution.py:19
  229.2 9.2 %collective-permute-done.13 = f32[4,64,384]{2,1,0:T(8,128)S(1)} collective-permute-done((f32[4,64,384]{2,1,0:T(8,128)S(1)}, f32[4,64,384]{2,1,0:T(8,128)S(1)}, u32[]{:S(2)}, u32[]{:S(2)}) %collective-permute-start.13) | collective-permute-done | bytes 393248 | tf_op jit(solution)/shard_map/ppermute | solution.py:16
  238.5 1.3 pad_maximum_fusion.14
  239.8 2.1 collective-permute-start.14
  241.9 0.0 copy-start.12
  241.9 5.4 %collective-permute-start.15 = (f32[40,4,384]{2,1,0:T(4,128)S(1)}, f32[40,4,384]{2,1,0:T(4,128)S(1)}, u32[]{:S(2)}, u32[]{:S(2)}) collective-permute-start(f32[40,4,384]{2,1,0:T(4,128)S(1)} %get-tuple-element.10), channel_id=1, source_target_pairs={{0,1},{1,2},{2,3},{4,5},{5,6},{6,7},{8,9},{9,10},{10,11},{12,13},{... | collective-permute-start | bytes 737288 | tf_op jit(solution)/shard_map/ppermute | solution.py:16
  247.4 1.4 collective-permute-done.14
  248.8 1.5 collective-permute-done.15
  250.3 3.7 pad_maximum_fusion.3
  254.0 32.6 %fusion.13 = f32[32,64,384]{2,1,0:T(8,128)} fusion(f32[32,64,384]{2,1,0:T(8,128)} %fusion.106, f32[4,64,384]{2,1,0:T(8,128)} %copy-done.7, f32[4,64,384]{2,1,0:T(8,128)S(1)} %collective-permute-done.12, f32[40,68,384]{2,1,0:T(8,128)} %get-tuple-element.8, f32[40,68,384]{2,1,0:T(8,128)S(1)} %get-tuple-element.7, f32[1,32,64,384]{3,2,1,0:T(8,128)} %param.14, ...), kind=kLoop, calls=%fused_computation.104 | loop fusion | flops 43253760 | bytes 51134464 | tf_op jit(solution)/shard_map/add | solution.py:109
  286.6 0.0 copy-start.8
  286.6 0.0 copy-start.9
  286.6 0.0 copy-start.10
  286.6 0.0 all-reduce.6.cloned.1.call-update
  286.6 80.5 %all-reduce.6.cloned.1.call-done = f32[32,64,384]{2,1,0:T(8,128)} async-done(((f32[32,64,384]{2,1,0:T(8,128)}), f32[32,64,384]{2,1,0:T(8,128)}) %all-reduce.6.cloned.1.call-update) | async-done | bytes 3145744 | tf_op jit(solution)/shard_map/psum | solution.py:113
  367.2 2.6 divide_add_fusion
  (32 shorter events, 0.1 us)
Async XLA Ops:
  7.2 42.4 %copy-start = (f32[1,32,64,384]{3,2,1,0:T(8,128)S(1)}, f32[1,32,64,384]{3,2,1,0:T(8,128)}, u32[]{:S(2)}) copy-start(f32[1,32,64,384]{3,2,1,0:T(8,128)} %param.15) | copy-start | bytes 9437188
  7.2 18.1 %copy-start.14 = (s32[1,3]{1,0:T(1,128)S(1)}, s32[1,3]{1,0:T(1,128)}, u32[]{:S(2)}) copy-start(s32[1,3]{1,0:T(1,128)} %param.20) | copy-start | bytes 40
  7.2 19.9 %copy-start.16 = (f32[1,2]{1,0:T(1,128)S(1)}, f32[1,2]{1,0:T(1,128)}, u32[]{:S(2)}) copy-start(f32[1,2]{1,0:T(1,128)} %param.21) | copy-start | bytes 28
  7.2 59.4 %all-gather.2.cloned.1.call-start = ((), (), s32[]{:S(2)}) async-start(), calls=%async_computation | async-start | bytes 3932160 | tf_op jit(solution)/shard_map/all_gather | solution.py:67
  7.9 359.2 %all-reduce.6.cloned.1.call-start = ((), (), s32[]{:S(2)}) async-start(), calls=%async_computation.1 | async-start | bytes 6291456 | tf_op jit(solution)/shard_map/psum | solution.py:113
  10.2 86.7 %collective-permute-start = (f32[4,64,384]{2,1,0:T(8,128)}, f32[4,64,384]{2,1,0:T(8,128)S(1)}, u32[]{:S(2)}, u32[]{:S(2)}) collective-permute-start(f32[4,64,384]{2,1,0:T(8,128)} %get-tuple-element.29), channel_id=1, source_target_pairs={{4,0},{8,4},{12,8},{16,12},{20,16},{24,20},{28,24},{5,1},{9,5},{13... | collective-permute-start | bytes 1179656 | tf_op jit(solution)/shard_map/ppermute | solution.py:19
  11.5 85.4 %collective-permute-start.1 = (f32[4,64,384]{2,1,0:T(8,128)}, f32[4,64,384]{2,1,0:T(8,128)}, u32[]{:S(2)}, u32[]{:S(2)}) collective-permute-start(f32[4,64,384]{2,1,0:T(8,128)} %get-tuple-element.30), channel_id=1, source_target_pairs={{0,4},{4,8},{8,12},{12,16},{16,20},{20,24},{24,28},{1,5},{5,9},{9,... | collective-permute-start | bytes 1179656 | tf_op jit(solution)/shard_map/ppermute | solution.py:16
  19.0 12.0 %collective-permute-start.4 = (f32[4,64,384]{2,1,0:T(8,128)}, f32[4,64,384]{2,1,0:T(8,128)}, u32[]{:S(2)}, u32[]{:S(2)}) collective-permute-start(f32[4,64,384]{2,1,0:T(8,128)} %get-tuple-element.27), channel_id=1, source_target_pairs={{4,0},{8,4},{12,8},{16,12},{20,16},{24,20},{28,24},{5,1},{9,5},{13... | collective-permute-start | bytes 1179656 | tf_op jit(solution)/shard_map/ppermute | solution.py:19
  20.3 29.2 %collective-permute-start.5 = (f32[4,64,384]{2,1,0:T(8,128)}, f32[4,64,384]{2,1,0:T(8,128)}, u32[]{:S(2)}, u32[]{:S(2)}) collective-permute-start(f32[4,64,384]{2,1,0:T(8,128)} %get-tuple-element.28), channel_id=1, source_target_pairs={{0,4},{4,8},{8,12},{12,16},{16,20},{20,24},{24,28},{1,5},{5,9},{9,... | collective-permute-start | bytes 1179656 | tf_op jit(solution)/shard_map/ppermute | solution.py:16
  26.5 40.2 %copy-start.15 = (pred[384]{0:T(512)(128)(4,1)}, pred[384]{0:T(512)(128)(4,1)S(1)}, u32[]{:S(2)}) copy-start(pred[384]{0:T(512)(128)(4,1)S(1)} %iota_compare_fusion.1) | copy-start | bytes 1156
  50.5 9.0 %collective-permute-start.6 = (f32[40,4,384]{2,1,0:T(4,128)S(1)}, f32[40,4,384]{2,1,0:T(4,128)S(1)}, u32[]{:S(2)}, u32[]{:S(2)}) collective-permute-start(f32[40,4,384]{2,1,0:T(4,128)S(1)} %get-tuple-element.17), channel_id=1, source_target_pairs={{1,0},{2,1},{3,2},{5,4},{6,5},{7,6},{9,8},{10,9},{11,10},{13,12},{... | collective-permute-start | bytes 737288 | tf_op jit(solution)/shard_map/ppermute | solution.py:19
  52.9 7.8 %collective-permute-start.7 = (f32[40,4,384]{2,1,0:T(4,128)S(1)}, f32[40,4,384]{2,1,0:T(4,128)S(1)}, u32[]{:S(2)}, u32[]{:S(2)}) collective-permute-start(f32[40,4,384]{2,1,0:T(4,128)S(1)} %get-tuple-element.18), channel_id=1, source_target_pairs={{0,1},{1,2},{2,3},{4,5},{5,6},{6,7},{8,9},{9,10},{10,11},{12,13},{... | collective-permute-start | bytes 737288 | tf_op jit(solution)/shard_map/ppermute | solution.py:16
  58.3 8.3 %copy-start.13 = (pred[32,64]{1,0:T(8,128)(4,1)}, pred[32,64]{1,0:T(8,128)(4,1)S(1)}, u32[]{:S(2)}) copy-start(pred[32,64]{1,0:T(8,128)(4,1)S(1)} %broadcast_and_fusion) | copy-start | bytes 6148
  90.1 19.0 %copy-start.1 = (f32[32,64,384]{2,1,0:T(8,128)S(1)}, f32[32,64,384]{2,1,0:T(8,128)}, u32[]{:S(2)}) copy-start(f32[32,64,384]{2,1,0:T(8,128)} %fusion.75) | copy-start | bytes 9437188
  91.5 17.7 %collective-permute-start.9 = (f32[4,64,384]{2,1,0:T(8,128)S(1)}, f32[4,64,384]{2,1,0:T(8,128)S(1)}, u32[]{:S(2)}, u32[]{:S(2)}) collective-permute-start(f32[4,64,384]{2,1,0:T(8,128)S(1)} %get-tuple-element.25), channel_id=1, source_target_pairs={{0,4},{4,8},{8,12},{12,16},{16,20},{20,24},{24,28},{1,5},{5,9},{9,... | collective-permute-start | bytes 1179656 | tf_op jit(solution)/shard_map/ppermute | solution.py:16
  95.6 13.5 %collective-permute-start.8 = (f32[4,64,384]{2,1,0:T(8,128)S(1)}, f32[4,64,384]{2,1,0:T(8,128)S(1)}, u32[]{:S(2)}, u32[]{:S(2)}) collective-permute-start(f32[4,64,384]{2,1,0:T(8,128)S(1)} %get-tuple-element.26), channel_id=1, source_target_pairs={{4,0},{8,4},{12,8},{16,12},{20,16},{24,20},{28,24},{5,1},{9,5},{13... | collective-permute-start | bytes 1179656 | tf_op jit(solution)/shard_map/ppermute | solution.py:19
  98.1 18.4 %copy-start.3 = (f32[1,32,64,384]{3,2,1,0:T(8,128)S(1)}, f32[1,32,64,384]{3,2,1,0:T(8,128)}, u32[]{:S(2)}) copy-start(f32[1,32,64,384]{3,2,1,0:T(8,128)} %param.17) | copy-start | bytes 9437188
  98.2 18.4 %collective-permute-start.2 = (f32[40,4,384]{2,1,0:T(4,128)S(1)}, f32[40,4,384]{2,1,0:T(4,128)S(1)}, u32[]{:S(2)}, u32[]{:S(2)}) collective-permute-start(f32[40,4,384]{2,1,0:T(4,128)S(1)} %get-tuple-element.21), channel_id=1, source_target_pairs={{1,0},{2,1},{3,2},{5,4},{6,5},{7,6},{9,8},{10,9},{11,10},{13,12},{... | collective-permute-start | bytes 737288 | tf_op jit(solution)/shard_map/ppermute | solution.py:19
  100.3 16.2 %collective-permute-start.3 = (f32[40,4,384]{2,1,0:T(4,128)S(1)}, f32[40,4,384]{2,1,0:T(4,128)S(1)}, u32[]{:S(2)}, u32[]{:S(2)}) collective-permute-start(f32[40,4,384]{2,1,0:T(4,128)S(1)} %get-tuple-element.22), channel_id=1, source_target_pairs={{0,1},{1,2},{2,3},{4,5},{5,6},{6,7},{8,9},{9,10},{10,11},{12,13},{... | collective-permute-start | bytes 737288 | tf_op jit(solution)/shard_map/ppermute | solution.py:16
  109.1 13.2 %copy-start.5 = (f32[4,64,384]{2,1,0:T(8,128)}, f32[4,64,384]{2,1,0:T(8,128)S(1)}, u32[]{:S(2)}) copy-start(f32[4,64,384]{2,1,0:T(8,128)S(1)} %collective-permute-done.9) | copy-start | bytes 1179652
  109.1 13.2 %copy-start.6 = (f32[4,64,384]{2,1,0:T(8,128)}, f32[4,64,384]{2,1,0:T(8,128)S(1)}, u32[]{:S(2)}) copy-start(f32[4,64,384]{2,1,0:T(8,128)S(1)} %collective-permute-done.8) | copy-start | bytes 1179652
  109.2 13.1 %collective-permute-start.10 = (f32[40,4,384]{2,1,0:T(4,128)S(1)}, f32[40,4,384]{2,1,0:T(4,128)S(1)}, u32[]{:S(2)}, u32[]{:S(2)}) collective-permute-start(f32[40,4,384]{2,1,0:T(4,128)S(1)} %get-tuple-element.13), channel_id=1, source_target_pairs={{1,0},{2,1},{3,2},{5,4},{6,5},{7,6},{9,8},{10,9},{11,10},{13,12},{... | collective-permute-start | bytes 737288 | tf_op jit(solution)/shard_map/ppermute | solution.py:19
  111.2 11.2 %collective-permute-start.11 = (f32[40,4,384]{2,1,0:T(4,128)S(1)}, f32[40,4,384]{2,1,0:T(4,128)S(1)}, u32[]{:S(2)}, u32[]{:S(2)}) collective-permute-start(f32[40,4,384]{2,1,0:T(4,128)S(1)} %get-tuple-element.14), channel_id=1, source_target_pairs={{0,1},{1,2},{2,3},{4,5},{5,6},{6,7},{8,9},{9,10},{10,11},{12,13},{... | collective-permute-start | bytes 737288 | tf_op jit(solution)/shard_map/ppermute | solution.py:16
  122.3 4.7 %copy-start.11 = (s32[1,32,64]{2,1,0:T(8,128)S(1)}, s32[1,32,64]{2,1,0:T(8,128)}, u32[]{:S(2)}) copy-start(s32[1,32,64]{2,1,0:T(8,128)} %param.19) | copy-start | bytes 24580
  217.2 33.1 %copy-start.4 = (f32[32,64,384]{2,1,0:T(8,128)S(1)}, f32[32,64,384]{2,1,0:T(8,128)}, u32[]{:S(2)}) copy-start(f32[32,64,384]{2,1,0:T(8,128)} %fusion.106) | copy-start | bytes 9437188
  218.5 10.7 %collective-permute-start.12 = (f32[4,64,384]{2,1,0:T(8,128)S(1)}, f32[4,64,384]{2,1,0:T(8,128)S(1)}, u32[]{:S(2)}, u32[]{:S(2)}) collective-permute-start(f32[4,64,384]{2,1,0:T(8,128)S(1)} %get-tuple-element.23), channel_id=1, source_target_pairs={{4,0},{8,4},{12,8},{16,12},{20,16},{24,20},{28,24},{5,1},{9,5},{13... | collective-permute-start | bytes 1179656 | tf_op jit(solution)/shard_map/ppermute | solution.py:19
  219.8 18.6 %collective-permute-start.13 = (f32[4,64,384]{2,1,0:T(8,128)S(1)}, f32[4,64,384]{2,1,0:T(8,128)S(1)}, u32[]{:S(2)}, u32[]{:S(2)}) collective-permute-start(f32[4,64,384]{2,1,0:T(8,128)S(1)} %get-tuple-element.24), channel_id=1, source_target_pairs={{0,4},{4,8},{8,12},{12,16},{16,20},{20,24},{24,28},{1,5},{5,9},{9,... | collective-permute-start | bytes 1179656 | tf_op jit(solution)/shard_map/ppermute | solution.py:16
  238.5 15.5 %copy-start.7 = (f32[4,64,384]{2,1,0:T(8,128)}, f32[4,64,384]{2,1,0:T(8,128)S(1)}, u32[]{:S(2)}) copy-start(f32[4,64,384]{2,1,0:T(8,128)S(1)} %collective-permute-done.13) | copy-start | bytes 1179652
  239.8 9.0 %collective-permute-start.14 = (f32[40,4,384]{2,1,0:T(4,128)S(1)}, f32[40,4,384]{2,1,0:T(4,128)S(1)}, u32[]{:S(2)}, u32[]{:S(2)}) collective-permute-start(f32[40,4,384]{2,1,0:T(4,128)S(1)} %get-tuple-element.9), channel_id=1, source_target_pairs={{1,0},{2,1},{3,2},{5,4},{6,5},{7,6},{9,8},{10,9},{11,10},{13,12},{... | collective-permute-start | bytes 737288 | tf_op jit(solution)/shard_map/ppermute | solution.py:19
  241.9 12.0 %copy-start.2 = (f32[32,64,384]{2,1,0:T(8,128)S(1)}, f32[32,64,384]{2,1,0:T(8,128)}, u32[]{:S(2)}) copy-start(f32[32,64,384]{2,1,0:T(8,128)} %fusion.75) | copy-start | bytes 9437188
  241.9 12.0 %copy-start.12 = (f32[32,64]{1,0:T(8,128)S(1)}, f32[32,64]{1,0:T(8,128)}, u32[]{:S(2)}) copy-start(f32[32,64]{1,0:T(8,128)} %get-tuple-element.31) | copy-start | bytes 24580
  241.9 8.3 %collective-permute-start.15 = (f32[40,4,384]{2,1,0:T(4,128)S(1)}, f32[40,4,384]{2,1,0:T(4,128)S(1)}, u32[]{:S(2)}, u32[]{:S(2)}) collective-permute-start(f32[40,4,384]{2,1,0:T(4,128)S(1)} %get-tuple-element.10), channel_id=1, source_target_pairs={{0,1},{1,2},{2,3},{4,5},{5,6},{6,7},{8,9},{9,10},{10,11},{12,13},{... | collective-permute-start | bytes 737288 | tf_op jit(solution)/shard_map/ppermute | solution.py:16
  286.6 80.6 %copy-start.8 = (f32[8,64,384]{2,1,0:T(8,128)S(1)}, f32[8,64,384]{2,1,0:T(8,128)}, u32[]{:S(2)}) copy-start(f32[8,64,384]{2,1,0:T(8,128)} %param.11) | copy-start | bytes 2359300
  286.6 80.6 %copy-start.9 = (f32[8,64,384]{2,1,0:T(8,128)S(1)}, f32[8,64,384]{2,1,0:T(8,128)}, u32[]{:S(2)}) copy-start(f32[8,64,384]{2,1,0:T(8,128)} %param.13) | copy-start | bytes 2359300
  286.6 80.6 %copy-start.10 = (f32[8,64,384]{2,1,0:T(8,128)S(1)}, f32[8,64,384]{2,1,0:T(8,128)}, u32[]{:S(2)}) copy-start(f32[8,64,384]{2,1,0:T(8,128)} %param.12) | copy-start | bytes 2359300
Sparse Core Ops, SparseCore 0:
  9.7 42.9 all-gather.1
  286.8 80.3 all-reduce.5
where the time goes:
time: 377 us
  other arithmetic  174 us (46%)
  waiting for transfers between devices  124 us (33%)
  starting transfers between devices  55 us (15%)
  between operations  14.4 us (4%)
  local copies, waits for them, and re-layouts  8.33 us (2%)
    psum x1, waiting for transfers between devices, on_device(): full_sum = lax.psum(imaging, 'shot')  80.5 us
    reduce_sum x1, other arithmetic, on_device(): misfit_early = jnp.sum(advanced * receiver_mask, axis=2) - observed[0, 0]  45.6 us
    add x1, other arithmetic, on_device(): 2.0 * adj_now - adj_later + stiffness * laplace(padded_adjoint)  43.2 us
    ppermute x8, starting transfers between devices, extended(): lax.ppermute(lax.slice_in_dim(block, block.shape[dim] - width, None, axis...  41.2 us
    add x1, other arithmetic, on_device(): adj_two * (farthest - 2.0 * advanced + present)  32.6 us
    ppermute x8, waiting for transfers between devices, extended(): lax.ppermute(lax.slice_in_dim(block, block.shape[dim] - width, None, axis...  32.4 us
    add x1, other arithmetic, on_device(): 2.0 * present - oldest + stiffness * laplace(padded_wave)  23.5 us
    concatenate x4, other arithmetic, extended(): block = jnp.concatenate([low, block, high], axis=dim)  20 us
  transfers between devices with their start and end apart: 18, of which 10 were waited for; matrix products, arithmetic and copies ran while one was open for 12% of the time, Pallas kernels for 0%

commit v1 on v0

--- a/solution.py
+++ b/solution.py
@@ -110,7 +110,7 @@
         advanced - 2.0 * present + oldest
     )
     share_rows = velocity.shape[0]
-    full_sum = lax.psum(imaging, "shot")
+    full_sum = jnp.sum(lax.all_gather(imaging, "shot"), axis=0)
     summed = lax.dynamic_slice_in_dim(full_sum, lax.axis_index("shot") * share_rows, share_rows, 0)
     gradient = 2.0 / velocity * summed
     p_half = momentum - 0.5 * leap_step * gradient

time: 377 us -> 425 us (1.13)
  waiting for transfers between devices: 124 us -> 167 us
  other arithmetic: 174 us -> 180 us
    all_gather x0 -> x1, waiting for transfers between devices: none -> 123 us  [on_device(): full_sum = jnp.sum(lax.all_gather(imaging, 'shot'), axis=0)]
    psum x1 -> x0, waiting for transfers between devices: 80.5 us -> none  [on_device(): full_sum = lax.psum(imaging, 'shot')]
    reduce_sum x0 -> x1, other arithmetic: none -> 6.14 us  [on_device(): full_sum = jnp.sum(lax.all_gather(imaging, 'shot'), axis=0)]
  transfers between devices with their start and end apart: 18 -> 18, of which waited for: 10 -> 10; matrix products, arithmetic and copies ran while one was open for 12% -> 11% of each run, Pallas kernels for 0% -> 0%
where the time goes in v1:
time: 425 us
  other arithmetic  180 us (42%)
  waiting for transfers between devices  167 us (39%)
  starting transfers between devices  55 us (13%)
  between operations  14.4 us (3%)
  local copies, waits for them, and re-layouts  8.35 us (2%)
    all_gather x1, waiting for transfers between devices, on_device(): full_sum = jnp.sum(lax.all_gather(imaging, 'shot'), axis=0)  123 us
    reduce_sum x1, other arithmetic, on_device(): misfit_early = jnp.sum(advanced * receiver_mask, axis=2) - observed[0, 0]  45.2 us
    add x1, other arithmetic, on_device(): 2.0 * adj_now - adj_later + stiffness * laplace(padded_adjoint)  43.3 us
    ppermute x8, starting transfers between devices, extended(): lax.ppermute(lax.slice_in_dim(block, block.shape[dim] - width, None, axis...  41.1 us
    add x1, other arithmetic, on_device(): adj_two * (farthest - 2.0 * advanced + present)  32.6 us
    ppermute x8, waiting for transfers between devices, extended(): lax.ppermute(lax.slice_in_dim(block, block.shape[dim] - width, None, axis...  32.4 us
    add x1, other arithmetic, on_device(): 2.0 * present - oldest + stiffness * laplace(padded_wave)  22.7 us
    concatenate x4, other arithmetic, extended(): block = jnp.concatenate([low, block, high], axis=dim)  19.9 us
  transfers between devices with their start and end apart: 18, of which 10 were waited for; matrix products, arithmetic and copies ran while one was open for 11% of the time, Pallas kernels for 0%

profile of v1, /device:TPU:1, one launch (start us, length us, event | category | flops | bytes accessed | tf_op | source)
XLA Modules:
  0.0 424.6 jit_solution(681743528998059546)
XLA Ops:
  7.2 0.0 copy-start
  7.2 0.0 all-gather.4.cloned.1.call-start
  7.2 0.7 all-gather.4.cloned.1.call-update
  7.9 0.0 all-gather.6.cloned.1.call-start
  8.0 2.2 slice_bitcast_fusion.3
  10.2 1.3 collective-permute-start
  11.5 5.4 %collective-permute-start.1 = (f32[4,64,384]{2,1,0:T(8,128)}, f32[4,64,384]{2,1,0:T(8,128)}, u32[]{:S(2)}, u32[]{:S(2)}) collective-permute-start(f32[4,64,384]{2,1,0:T(8,128)} %get-tuple-element.30), channel_id=1, source_target_pairs={{0,4},{4,8},{8,12},{12,16},{16,20},{20,24},{24,28},{1,5},{5,9},{9,... | collective-permute-start | bytes 1179656 | tf_op jit(solution)/shard_map/ppermute | solution.py:16
  16.9 2.1 slice_bitcast_fusion.1
  19.0 1.3 collective-permute-start.4
  20.3 4.9 %collective-permute-start.5 = (f32[4,64,384]{2,1,0:T(8,128)}, f32[4,64,384]{2,1,0:T(8,128)}, u32[]{:S(2)}, u32[]{:S(2)}) collective-permute-start(f32[4,64,384]{2,1,0:T(8,128)} %get-tuple-element.28), channel_id=1, source_target_pairs={{0,4},{4,8},{8,12},{12,16},{16,20},{20,24},{24,28},{1,5},{5,9},{9,... | collective-permute-start | bytes 1179656 | tf_op jit(solution)/shard_map/ppermute | solution.py:16
  25.2 0.7 fusion.146
  25.9 0.6 iota_compare_fusion.1
  26.5 0.7 add_compare_fusion.1
  27.2 0.6 fusion.145
  27.9 3.1 collective-permute-done.4
  31.0 18.5 %collective-permute-done.5 = f32[4,64,384]{2,1,0:T(8,128)} collective-permute-done((f32[4,64,384]{2,1,0:T(8,128)}, f32[4,64,384]{2,1,0:T(8,128)}, u32[]{:S(2)}, u32[]{:S(2)}) %collective-permute-start.5) | collective-permute-done | bytes 393248 | tf_op jit(solution)/shard_map/ppermute | solution.py:16
  49.5 1.0 pad_maximum_fusion.20
  50.5 2.4 collective-permute-start.6
  52.9 4.7 %collective-permute-start.7 = (f32[40,4,384]{2,1,0:T(4,128)S(1)}, f32[40,4,384]{2,1,0:T(4,128)S(1)}, u32[]{:S(2)}, u32[]{:S(2)}) collective-permute-start(f32[40,4,384]{2,1,0:T(4,128)S(1)} %get-tuple-element.18), channel_id=1, source_target_pairs={{0,1},{1,2},{2,3},{4,5},{5,6},{6,7},{8,9},{9,10},{10,11},{12,13},{... | collective-permute-start | bytes 737288 | tf_op jit(solution)/shard_map/ppermute | solution.py:16
  57.6 0.6 add_compare_fusion
  58.2 0.1 broadcast_and_fusion
  58.3 1.2 collective-permute-done.6
  59.5 1.2 collective-permute-done.7
  60.7 5.9 %pad_maximum_fusion.1 = (f32[40,68,384]{2,1,0:T(8,128)}, f32[40,68,384]{2,1,0:T(8,128)}) fusion(f32[40,4,384]{2,1,0:T(4,128)S(1)} %collective-permute-done.6, f32[4,64,384]{2,1,0:T(8,128)} %collective-permute-done.4, f32[32,64,384]{2,1,0:T(8,128)S(1)} %bitcast.37, f32[4,64,384]{2,1,0:T(8,128)} %collective-permute-done.5, ...), kind=kLoop, calls=%fused_computation.59 | loop fusion | flops 6266880 | bytes 12779520 | tf_op jit(solution)/shard_map/concatenate | solution.py:20
  66.6 22.7 %fusion.75 = f32[32,64,384]{2,1,0:T(8,128)} fusion(f32[32,64,384]{2,1,0:T(8,128)S(1)} %bitcast.38, f32[4,64,384]{2,1,0:T(8,128)} %collective-permute-done.5, f32[4,64,384]{2,1,0:T(8,128)} %collective-permute-done.4, f32[40,68,384]{2,1,0:T(8,128)} %get-tuple-element.16, f32[40,68,384]{2,1,0:T(8,128)} %get-tuple-element.15, f32[1,32,64,384]{3,2,1,0:T(8,128)} %param.14, ...), kind=kLoop, calls=%fused_computation.166 | loop fusion | flops 36175872 | bytes 38537604 | tf_op jit(solution)/shard_map/add | solution.py:86
  89.3 1.3 fusion.144
  90.6 4.1 collective-permute-start.9
  94.8 1.3 collective-permute-start.8
  96.1 0.0 collective-permute-done
  96.1 0.0 collective-permute-done.1
  96.1 1.2 pad_maximum_fusion.23
  97.3 0.0 copy-start.3
  97.3 2.2 collective-permute-start.2
  99.5 6.8 %collective-permute-start.3 = (f32[40,4,384]{2,1,0:T(4,128)S(1)}, f32[40,4,384]{2,1,0:T(4,128)S(1)}, u32[]{:S(2)}, u32[]{:S(2)}) collective-permute-start(f32[40,4,384]{2,1,0:T(4,128)S(1)} %get-tuple-element.22), channel_id=1, source_target_pairs={{0,1},{1,2},{2,3},{4,5},{5,6},{6,7},{8,9},{9,10},{10,11},{12,13},{... | collective-permute-start | bytes 737288 | tf_op jit(solution)/shard_map/ppermute | solution.py:16
  106.3 2.0 collective-permute-done.9
  108.3 0.0 collective-permute-done.8
  108.3 0.1 pad_maximum_fusion.17
  108.4 1.9 collective-permute-start.10
  110.3 5.3 %collective-permute-start.11 = (f32[40,4,384]{2,1,0:T(4,128)S(1)}, f32[40,4,384]{2,1,0:T(4,128)S(1)}, u32[]{:S(2)}, u32[]{:S(2)}) collective-permute-start(f32[40,4,384]{2,1,0:T(4,128)S(1)} %get-tuple-element.14), channel_id=1, source_target_pairs={{0,1},{1,2},{2,3},{4,5},{5,6},{6,7},{8,9},{9,10},{10,11},{12,13},{... | collective-permute-start | bytes 737288 | tf_op jit(solution)/shard_map/ppermute | solution.py:16
  115.7 0.0 collective-permute-done.2
  115.7 0.0 collective-permute-done.3
  115.7 5.7 %pad_maximum_fusion = (f32[40,68,384]{2,1,0:T(8,128)}, f32[40,68,384]{2,1,0:T(8,128)}) fusion(f32[40,4,384]{2,1,0:T(4,128)S(1)} %collective-permute-done.2, f32[4,64,384]{2,1,0:T(8,128)S(1)} %collective-permute-done, f32[32,64,384]{2,1,0:T(8,128)S(1)} %bitcast.41, f32[4,64,384]{2,1,0:T(8,128)} %collective-permute-done.1, ...), kind=kLoop, calls=%fused_computation.57 | loop fusion | flops 6266880 | bytes 12779520 | tf_op jit(solution)/shard_map/concatenate | solution.py:20
  121.4 0.0 collective-permute-done.11
  121.4 4.7 %pad_maximum_fusion.2 = (f32[40,68,384]{2,1,0:T(8,128)}, f32[40,68,384]{2,1,0:T(8,128)}) fusion(f32[40,4,384]{2,1,0:T(4,128)S(1)} %collective-permute-done.10, f32[4,64,384]{2,1,0:T(8,128)S(1)} %collective-permute-done.8, f32[32,64,384]{2,1,0:T(8,128)S(1)} %copy-done.1, f32[4,64,384]{2,1,0:T(8,128)S(1)} %collective-permute-done.9, ...), kind=kLoop, calls=%fused_computation.61 | loop fusion | flops 6266880 | bytes 12779520 | tf_op jit(solution)/shard_map/concatenate | solution.py:20
  126.1 45.2 %select_reduce_fusion = (f32[32,64]{1,0:T(8,128)}, f32[32,64]{1,0:T(8,128)}, f32[32,64,384]{2,1,0:T(8,128)}) fusion(f32[32,64,384]{2,1,0:T(8,128)} %fusion.75, s32[32,64]{1,0:T(8,128)S(1)} %bitcast.43, f32[]{:T(128)} %bitcast.13, pred[384]{0:T(512)(128)(4,1)} %copy-done.12, pred[32,64]{1,0:T(8,128)(4,1)} %copy-done.10, ...), kind=kLoop, calls=%fused_computation.252 | loop fusion | flops 40103936 | bytes 38562180 | tf_op jit(solution)/shard_map/reduce_sum | solution.py:96
  171.3 1.4 bitcast_subtract_fusion.2
  172.7 43.3 %fusion.106 = f32[32,64,384]{2,1,0:T(8,128)} fusion(f32[32,64,384]{2,1,0:T(8,128)} %bitcast.40, f32[4,64,384]{2,1,0:T(8,128)} %collective-permute-done.1, f32[4,64,384]{2,1,0:T(8,128)S(1)} %collective-permute-done, f32[40,68,384]{2,1,0:T(8,128)} %get-tuple-element.20, f32[40,68,384]{2,1,0:T(8,128)} %get-tuple-element.19, f32[1,32,64,384]{3,2,1,0:T(8,128)} %param.16, ...), kind=kLoop, calls=%fused_computation.197 | loop fusion | flops 36175872 | bytes 38551552 | tf_op jit(solution)/shard_map/add | solution.py:98
  216.0 1.3 fusion.143
  217.3 1.3 collective-permute-start.12
  218.6 4.5 %collective-permute-start.13 = (f32[4,64,384]{2,1,0:T(8,128)S(1)}, f32[4,64,384]{2,1,0:T(8,128)S(1)}, u32[]{:S(2)}, u32[]{:S(2)}) collective-permute-start(f32[4,64,384]{2,1,0:T(8,128)S(1)} %get-tuple-element.24), channel_id=1, source_target_pairs={{0,4},{4,8},{8,12},{12,16},{16,20},{20,24},{24,28},{1,5},{5,9},{9,... | collective-permute-start | bytes 1179656 | tf_op jit(solution)/shard_map/ppermute | solution.py:16
  223.1 4.9 %collective-permute-done.12 = f32[4,64,384]{2,1,0:T(8,128)S(1)} collective-permute-done((f32[4,64,384]{2,1,0:T(8,128)S(1)}, f32[4,64,384]{2,1,0:T(8,128)S(1)}, u32[]{:S(2)}, u32[]{:S(2)}) %collective-permute-start.12) | collective-permute-done | bytes 393248 | tf_op jit(solution)/shard_map/ppermute | solution.py:19
  228.0 9.2 %collective-permute-done.13 = f32[4,64,384]{2,1,0:T(8,128)S(1)} collective-permute-done((f32[4,64,384]{2,1,0:T(8,128)S(1)}, f32[4,64,384]{2,1,0:T(8,128)S(1)}, u32[]{:S(2)}, u32[]{:S(2)}) %collective-permute-start.13) | collective-permute-done | bytes 393248 | tf_op jit(solution)/shard_map/ppermute | solution.py:16
  237.2 1.3 pad_maximum_fusion.14
  238.6 2.1 collective-permute-start.14
  240.7 0.0 copy-start.9
  240.7 5.4 %collective-permute-start.15 = (f32[40,4,384]{2,1,0:T(4,128)S(1)}, f32[40,4,384]{2,1,0:T(4,128)S(1)}, u32[]{:S(2)}, u32[]{:S(2)}) collective-permute-start(f32[40,4,384]{2,1,0:T(4,128)S(1)} %get-tuple-element.10), channel_id=1, source_target_pairs={{0,1},{1,2},{2,3},{4,5},{5,6},{6,7},{8,9},{9,10},{10,11},{12,13},{... | collective-permute-start | bytes 737288 | tf_op jit(solution)/shard_map/ppermute | solution.py:16
  246.2 1.4 collective-permute-done.14
  247.6 1.5 collective-permute-done.15
  249.1 3.7 pad_maximum_fusion.3
  252.7 32.6 %fusion.13 = f32[32,64,384]{2,1,0:T(8,128)} fusion(f32[32,64,384]{2,1,0:T(8,128)} %fusion.106, f32[4,64,384]{2,1,0:T(8,128)} %copy-done.7, f32[4,64,384]{2,1,0:T(8,128)S(1)} %collective-permute-done.12, f32[40,68,384]{2,1,0:T(8,128)} %get-tuple-element.8, f32[40,68,384]{2,1,0:T(8,128)S(1)} %get-tuple-element.7, f32[1,32,64,384]{3,2,1,0:T(8,128)} %param.14, ...), kind=kLoop, calls=%fused_computation.104 | loop fusion | flops 43253760 | bytes 51134464 | tf_op jit(solution)/shard_map/add | solution.py:109
  285.4 0.0 all-gather.6.cloned.1.call-update
  285.4 123.1 %all-gather.6.cloned.1.call-done = f32[128,64,384]{2,1,0:T(8,128)} async-done(((f32[32,64,384]{2,1,0:T(8,128)}), f32[128,64,384]{2,1,0:T(8,128)}) %all-gather.6.cloned.1.call-update) | async-done | bytes 12582928 | tf_op jit(solution)/shard_map/all_gather | solution.py:113
  408.5 6.1 %reduce_sum.29 = f32[32,64,384]{2,1,0:T(8,128)S(1)} reduce(f32[4,32,64,384]{3,2,1,0:T(8,128)} %bitcast.42, f32[]{:T(128)} %constant.14.clone.1), dimensions={0}, to_apply=%region_2.3 | reduce | flops 2359296 | bytes 15728644 | tf_op jit(solution)/shard_map/reduce_sum | solution.py:113
  414.7 3.0 divide_add_fusion
  (27 shorter events, 0.1 us)
Async XLA Ops:
  7.2 42.4 %copy-start = (f32[1,32,64,384]{3,2,1,0:T(8,128)S(1)}, f32[1,32,64,384]{3,2,1,0:T(8,128)}, u32[]{:S(2)}) copy-start(f32[1,32,64,384]{3,2,1,0:T(8,128)} %param.15) | copy-start | bytes 9437188
  7.2 18.0 %copy-start.11 = (s32[1,3]{1,0:T(1,128)S(1)}, s32[1,3]{1,0:T(1,128)}, u32[]{:S(2)}) copy-start(s32[1,3]{1,0:T(1,128)} %param.20) | copy-start | bytes 40
  7.2 20.0 %copy-start.13 = (f32[1,2]{1,0:T(1,128)S(1)}, f32[1,2]{1,0:T(1,128)}, u32[]{:S(2)}) copy-start(f32[1,2]{1,0:T(1,128)} %param.21) | copy-start | bytes 28
  7.2 59.4 %all-gather.4.cloned.1.call-start = ((), (), s32[]{:S(2)}) async-start(), calls=%async_computation | async-start | bytes 3932160 | tf_op jit(solution)/shard_map/all_gather | solution.py:67
  7.9 400.6 %all-gather.6.cloned.1.call-start = ((), (), s32[]{:S(2)}) async-start(), calls=%async_computation.1 | async-start | bytes 15728640 | tf_op jit(solution)/shard_map/all_gather | solution.py:113
  10.2 85.9 %collective-permute-start = (f32[4,64,384]{2,1,0:T(8,128)}, f32[4,64,384]{2,1,0:T(8,128)S(1)}, u32[]{:S(2)}, u32[]{:S(2)}) collective-permute-start(f32[4,64,384]{2,1,0:T(8,128)} %get-tuple-element.29), channel_id=1, source_target_pairs={{4,0},{8,4},{12,8},{16,12},{20,16},{24,20},{28,24},{5,1},{9,5},{13... | collective-permute-start | bytes 1179656 | tf_op jit(solution)/shard_map/ppermute | solution.py:19
  11.5 84.6 %collective-permute-start.1 = (f32[4,64,384]{2,1,0:T(8,128)}, f32[4,64,384]{2,1,0:T(8,128)}, u32[]{:S(2)}, u32[]{:S(2)}) collective-permute-start(f32[4,64,384]{2,1,0:T(8,128)} %get-tuple-element.30), channel_id=1, source_target_pairs={{0,4},{4,8},{8,12},{12,16},{16,20},{20,24},{24,28},{1,5},{5,9},{9,... | collective-permute-start | bytes 1179656 | tf_op jit(solution)/shard_map/ppermute | solution.py:16
  19.0 12.0 %collective-permute-start.4 = (f32[4,64,384]{2,1,0:T(8,128)}, f32[4,64,384]{2,1,0:T(8,128)}, u32[]{:S(2)}, u32[]{:S(2)}) collective-permute-start(f32[4,64,384]{2,1,0:T(8,128)} %get-tuple-element.27), channel_id=1, source_target_pairs={{4,0},{8,4},{12,8},{16,12},{20,16},{24,20},{28,24},{5,1},{9,5},{13... | collective-permute-start | bytes 1179656 | tf_op jit(solution)/shard_map/ppermute | solution.py:19
  20.3 29.2 %collective-permute-start.5 = (f32[4,64,384]{2,1,0:T(8,128)}, f32[4,64,384]{2,1,0:T(8,128)}, u32[]{:S(2)}, u32[]{:S(2)}) collective-permute-start(f32[4,64,384]{2,1,0:T(8,128)} %get-tuple-element.28), channel_id=1, source_target_pairs={{0,4},{4,8},{8,12},{12,16},{16,20},{20,24},{24,28},{1,5},{5,9},{9,... | collective-permute-start | bytes 1179656 | tf_op jit(solution)/shard_map/ppermute | solution.py:16
  26.5 40.1 %copy-start.12 = (pred[384]{0:T(512)(128)(4,1)}, pred[384]{0:T(512)(128)(4,1)S(1)}, u32[]{:S(2)}) copy-start(pred[384]{0:T(512)(128)(4,1)S(1)} %iota_compare_fusion.1) | copy-start | bytes 1156
  50.5 9.0 %collective-permute-start.6 = (f32[40,4,384]{2,1,0:T(4,128)S(1)}, f32[40,4,384]{2,1,0:T(4,128)S(1)}, u32[]{:S(2)}, u32[]{:S(2)}) collective-permute-start(f32[40,4,384]{2,1,0:T(4,128)S(1)} %get-tuple-element.17), channel_id=1, source_target_pairs={{1,0},{2,1},{3,2},{5,4},{6,5},{7,6},{9,8},{10,9},{11,10},{13,12},{... | collective-permute-start | bytes 737288 | tf_op jit(solution)/shard_map/ppermute | solution.py:19
  52.9 7.8 %collective-permute-start.7 = (f32[40,4,384]{2,1,0:T(4,128)S(1)}, f32[40,4,384]{2,1,0:T(4,128)S(1)}, u32[]{:S(2)}, u32[]{:S(2)}) collective-permute-start(f32[40,4,384]{2,1,0:T(4,128)S(1)} %get-tuple-element.18), channel_id=1, source_target_pairs={{0,1},{1,2},{2,3},{4,5},{5,6},{6,7},{8,9},{9,10},{10,11},{12,13},{... | collective-permute-start | bytes 737288 | tf_op jit(solution)/shard_map/ppermute | solution.py:16
  58.3 8.3 %copy-start.10 = (pred[32,64]{1,0:T(8,128)(4,1)}, pred[32,64]{1,0:T(8,128)(4,1)S(1)}, u32[]{:S(2)}) copy-start(pred[32,64]{1,0:T(8,128)(4,1)S(1)} %broadcast_and_fusion) | copy-start | bytes 6148
  89.3 19.0 %copy-start.1 = (f32[32,64,384]{2,1,0:T(8,128)S(1)}, f32[32,64,384]{2,1,0:T(8,128)}, u32[]{:S(2)}) copy-start(f32[32,64,384]{2,1,0:T(8,128)} %fusion.75) | copy-start | bytes 9437188
  90.6 17.7 %collective-permute-start.9 = (f32[4,64,384]{2,1,0:T(8,128)S(1)}, f32[4,64,384]{2,1,0:T(8,128)S(1)}, u32[]{:S(2)}, u32[]{:S(2)}) collective-permute-start(f32[4,64,384]{2,1,0:T(8,128)S(1)} %get-tuple-element.25), channel_id=1, source_target_pairs={{0,4},{4,8},{8,12},{12,16},{16,20},{20,24},{24,28},{1,5},{5,9},{9,... | collective-permute-start | bytes 1179656 | tf_op jit(solution)/shard_map/ppermute | solution.py:16
  94.8 13.5 %collective-permute-start.8 = (f32[4,64,384]{2,1,0:T(8,128)S(1)}, f32[4,64,384]{2,1,0:T(8,128)S(1)}, u32[]{:S(2)}, u32[]{:S(2)}) collective-permute-start(f32[4,64,384]{2,1,0:T(8,128)S(1)} %get-tuple-element.26), channel_id=1, source_target_pairs={{4,0},{8,4},{12,8},{16,12},{20,16},{24,20},{28,24},{5,1},{9,5},{13... | collective-permute-start | bytes 1179656 | tf_op jit(solution)/shard_map/ppermute | solution.py:19
  97.3 18.4 %copy-start.3 = (f32[1,32,64,384]{3,2,1,0:T(8,128)S(1)}, f32[1,32,64,384]{3,2,1,0:T(8,128)}, u32[]{:S(2)}) copy-start(f32[1,32,64,384]{3,2,1,0:T(8,128)} %param.17) | copy-start | bytes 9437188
  97.3 18.4 %collective-permute-start.2 = (f32[40,4,384]{2,1,0:T(4,128)S(1)}, f32[40,4,384]{2,1,0:T(4,128)S(1)}, u32[]{:S(2)}, u32[]{:S(2)}) collective-permute-start(f32[40,4,384]{2,1,0:T(4,128)S(1)} %get-tuple-element.21), channel_id=1, source_target_pairs={{1,0},{2,1},{3,2},{5,4},{6,5},{7,6},{9,8},{10,9},{11,10},{13,12},{... | collective-permute-start | bytes 737288 | tf_op jit(solution)/shard_map/ppermute | solution.py:19
  99.5 16.2 %collective-permute-start.3 = (f32[40,4,384]{2,1,0:T(4,128)S(1)}, f32[40,4,384]{2,1,0:T(4,128)S(1)}, u32[]{:S(2)}, u32[]{:S(2)}) collective-permute-start(f32[40,4,384]{2,1,0:T(4,128)S(1)} %get-tuple-element.22), channel_id=1, source_target_pairs={{0,1},{1,2},{2,3},{4,5},{5,6},{6,7},{8,9},{9,10},{10,11},{12,13},{... | collective-permute-start | bytes 737288 | tf_op jit(solution)/shard_map/ppermute | solution.py:16
  108.3 13.1 %copy-start.5 = (f32[4,64,384]{2,1,0:T(8,128)}, f32[4,64,384]{2,1,0:T(8,128)S(1)}, u32[]{:S(2)}) copy-start(f32[4,64,384]{2,1,0:T(8,128)S(1)} %collective-permute-done.9) | copy-start | bytes 1179652
  108.3 13.1 %copy-start.6 = (f32[4,64,384]{2,1,0:T(8,128)}, f32[4,64,384]{2,1,0:T(8,128)S(1)}, u32[]{:S(2)}) copy-start(f32[4,64,384]{2,1,0:T(8,128)S(1)} %collective-permute-done.8) | copy-start | bytes 1179652
  108.4 13.0 %collective-permute-start.10 = (f32[40,4,384]{2,1,0:T(4,128)S(1)}, f32[40,4,384]{2,1,0:T(4,128)S(1)}, u32[]{:S(2)}, u32[]{:S(2)}) collective-permute-start(f32[40,4,384]{2,1,0:T(4,128)S(1)} %get-tuple-element.13), channel_id=1, source_target_pairs={{1,0},{2,1},{3,2},{5,4},{6,5},{7,6},{9,8},{10,9},{11,10},{13,12},{... | collective-permute-start | bytes 737288 | tf_op jit(solution)/shard_map/ppermute | solution.py:19
  110.3 11.1 %collective-permute-start.11 = (f32[40,4,384]{2,1,0:T(4,128)S(1)}, f32[40,4,384]{2,1,0:T(4,128)S(1)}, u32[]{:S(2)}, u32[]{:S(2)}) collective-permute-start(f32[40,4,384]{2,1,0:T(4,128)S(1)} %get-tuple-element.14), channel_id=1, source_target_pairs={{0,1},{1,2},{2,3},{4,5},{5,6},{6,7},{8,9},{9,10},{10,11},{12,13},{... | collective-permute-start | bytes 737288 | tf_op jit(solution)/shard_map/ppermute | solution.py:16
  121.4 4.7 %copy-start.8 = (s32[1,32,64]{2,1,0:T(8,128)S(1)}, s32[1,32,64]{2,1,0:T(8,128)}, u32[]{:S(2)}) copy-start(s32[1,32,64]{2,1,0:T(8,128)} %param.19) | copy-start | bytes 24580
  216.0 33.1 %copy-start.4 = (f32[32,64,384]{2,1,0:T(8,128)S(1)}, f32[32,64,384]{2,1,0:T(8,128)}, u32[]{:S(2)}) copy-start(f32[32,64,384]{2,1,0:T(8,128)} %fusion.106) | copy-start | bytes 9437188
  217.3 10.7 %collective-permute-start.12 = (f32[4,64,384]{2,1,0:T(8,128)S(1)}, f32[4,64,384]{2,1,0:T(8,128)S(1)}, u32[]{:S(2)}, u32[]{:S(2)}) collective-permute-start(f32[4,64,384]{2,1,0:T(8,128)S(1)} %get-tuple-element.23), channel_id=1, source_target_pairs={{4,0},{8,4},{12,8},{16,12},{20,16},{24,20},{28,24},{5,1},{9,5},{13... | collective-permute-start | bytes 1179656 | tf_op jit(solution)/shard_map/ppermute | solution.py:19
  218.6 18.6 %collective-permute-start.13 = (f32[4,64,384]{2,1,0:T(8,128)S(1)}, f32[4,64,384]{2,1,0:T(8,128)S(1)}, u32[]{:S(2)}, u32[]{:S(2)}) collective-permute-start(f32[4,64,384]{2,1,0:T(8,128)S(1)} %get-tuple-element.24), channel_id=1, source_target_pairs={{0,4},{4,8},{8,12},{12,16},{16,20},{20,24},{24,28},{1,5},{5,9},{9,... | collective-permute-start | bytes 1179656 | tf_op jit(solution)/shard_map/ppermute | solution.py:16
  237.2 15.5 %copy-start.7 = (f32[4,64,384]{2,1,0:T(8,128)}, f32[4,64,384]{2,1,0:T(8,128)S(1)}, u32[]{:S(2)}) copy-start(f32[4,64,384]{2,1,0:T(8,128)S(1)} %collective-permute-done.13) | copy-start | bytes 1179652
  238.6 9.0 %collective-permute-start.14 = (f32[40,4,384]{2,1,0:T(4,128)S(1)}, f32[40,4,384]{2,1,0:T(4,128)S(1)}, u32[]{:S(2)}, u32[]{:S(2)}) collective-permute-start(f32[40,4,384]{2,1,0:T(4,128)S(1)} %get-tuple-element.9), channel_id=1, source_target_pairs={{1,0},{2,1},{3,2},{5,4},{6,5},{7,6},{9,8},{10,9},{11,10},{13,12},{... | collective-permute-start | bytes 737288 | tf_op jit(solution)/shard_map/ppermute | solution.py:19
  240.7 12.0 %copy-start.2 = (f32[32,64,384]{2,1,0:T(8,128)S(1)}, f32[32,64,384]{2,1,0:T(8,128)}, u32[]{:S(2)}) copy-start(f32[32,64,384]{2,1,0:T(8,128)} %fusion.75) | copy-start | bytes 9437188
  240.7 12.0 %copy-start.9 = (f32[32,64]{1,0:T(8,128)S(1)}, f32[32,64]{1,0:T(8,128)}, u32[]{:S(2)}) copy-start(f32[32,64]{1,0:T(8,128)} %get-tuple-element.31) | copy-start | bytes 24580
  240.7 8.3 %collective-permute-start.15 = (f32[40,4,384]{2,1,0:T(4,128)S(1)}, f32[40,4,384]{2,1,0:T(4,128)S(1)}, u32[]{:S(2)}, u32[]{:S(2)}) collective-permute-start(f32[40,4,384]{2,1,0:T(4,128)S(1)} %get-tuple-element.10), channel_id=1, source_target_pairs={{0,1},{1,2},{2,3},{4,5},{5,6},{6,7},{8,9},{9,10},{10,11},{12,13},{... | collective-permute-start | bytes 737288 | tf_op jit(solution)/shard_map/ppermute | solution.py:16
Sparse Core Ops, SparseCore 0:
  9.7 42.9 all-gather.3
  285.5 122.9 all-gather.5
